TPU v7x, 32 devices: a whole 2x2x4 slice. The times are simulated.
32 devices in a mesh: shard: 2 (over y), context: 4 (over x, core), tensor: 4 (over z).
Axes of the slice: x: 2, y: 2, z: 4, core: 2. Of those that a mesh axis runs over, the one named last changes fastest.
Arguments:
- tokens: bfloat16 [5120, 1088], P(('shard', 'context', 'tensor')), may hold values from -6 to 6
- segments: int32 [2, 2560], P('shard', ('context', 'tensor')), may hold values from 0 to 5, never falling along the last dimension, each value on 1 to 1920 neighbouring positions
- w_qkv: bfloat16 [1088, 3264], P('shard'), may hold values from -0.1875 to 0.1875
- w_out: bfloat16 [1088, 1088], P('shard'), may hold values from -1.5 to 1.5
- ln1_gain: bfloat16 [1088], P('shard'), may hold values from 0.5 to 1.5
- ln1_bias: bfloat16 [1088], P('shard'), may hold values from -3 to 3
- ln2_gain: bfloat16 [1088], P('shard'), may hold values from 0.5 to 1.5
- ln2_bias: bfloat16 [1088], P('shard'), may hold values from -3 to 3
- w_up: bfloat16 [1088, 4352], P('shard', 'tensor'), may hold values from -0.1875 to 0.1875
- w_down: bfloat16 [4352, 1088], P('tensor', 'shard'), may hold values from -0.09375 to 0.09375
- out_grad: bfloat16 [5120, 1088], P(('shard', 'context', 'tensor')), may hold values from -6 to 6
Outputs:
- result: bfloat16 [5120, 1088], P(('shard', 'context', 'tensor'))
- input_grad: bfloat16 [5120, 1088], P(('shard', 'context', 'tensor'))
- grad_w_qkv: float32 [1088, 3264], P('shard')
- grad_w_out: float32 [1088, 1088], P('shard')
- grad_ln1_gain: float32 [1088], P('shard')
- grad_ln1_bias: float32 [1088], P('shard')
- grad_ln2_gain: float32 [1088], P('shard')
- grad_ln2_bias: float32 [1088], P('shard')
- grad_w_up: float32 [1088, 4352], P('shard', 'tensor')
- grad_w_down: float32 [4352, 1088], P('tensor', 'shard')
Inputs may be any that keep to these rules, and one draw needn't show every extreme that they name: `segments`: row s lists the sequence numbers of the 2560 tokens of shard index s in order; they never fall, each of the 6 sequences has 1 to 1920 tokens, and one has exactly 1920.
All inputs are finite; a program needn't handle non-finite values.
Results may differ from a plain program's by a relative error of at most 0.012.
Values may be sent and summed in bfloat16 or wider, within the bound.
No kernel may reach another device: no remote copies, remote signals or barrier semaphores. Data moves between devices by JAX's collectives and lax.ppermute only.
A program may use at most 192 MiB of HBM per device.

v0:
```python
import math

import jax
import jax.numpy as jnp
from jax import lax
from jax.sharding import PartitionSpec as P

HEADS = 17
HEAD_DIM = 64


EPSILON = 1e-05


def layer_norm(values, gain, shift):
    average = jnp.mean(values, axis=-1, keepdims=True)
    centred = values - average
    variance = jnp.mean(centred * centred, axis=-1, keepdims=True)
    return centred * lax.rsqrt(variance + EPSILON) * gain + shift


def head_cols(matrix, head_id):
    return lax.dynamic_slice_in_dim(matrix, head_id * HEAD_DIM, HEAD_DIM, 1)


def outer_rows(left, right):
    return lax.dot_general(
        left, right, (((1,), (1,)), ((), ())), preferred_element_type=jnp.float32
    )


def inner_rows(left, right):
    return lax.dot_general(
        left, right, (((0,), (0,)), ((), ())), preferred_element_type=jnp.float32
    )


def join_heads(stacked):
    return stacked.transpose(1, 0, 2).reshape(stacked.shape[1], -1)


def make_mask(query_pos, query_seq, key_pos, key_seq):
    return (key_pos[None, :] <= query_pos[:, None]) & (key_seq[None, :] == query_seq[:, None])


def attend_forward(queries, keys, values, allowed, scale):

    def one_head(running, head_id):
        scores = outer_rows(head_cols(queries, head_id), head_cols(keys, head_id)) * scale
        scores = jnp.where(allowed, scores, -1e30)
        highest = jnp.max(scores, axis=1, keepdims=True)
        log_total = highest + jnp.log(jnp.sum(jnp.exp(scores - highest), axis=1, keepdims=True))
        shares = jnp.exp(scores - log_total).astype(jnp.bfloat16)
        joined = jnp.dot(shares, head_cols(values, head_id), preferred_element_type=jnp.float32)
        return (running, (joined, log_total[:, 0]))

    unused, (outputs, totals) = lax.scan(one_head, 0, jnp.arange(HEADS))
    return (join_heads(outputs), totals)


def attend_backward(queries, keys, values, allowed, grad_out, totals, scale):

    def one_head(running, head_id):
        q_head = head_cols(queries, head_id)
        k_head = head_cols(keys, head_id)
        v_head = head_cols(values, head_id)
        g_head = head_cols(grad_out, head_id)
        scores = jnp.where(allowed, outer_rows(q_head, k_head) * scale, -1e30)
        shares = jnp.exp(scores - totals[head_id][:, None])
        d_shares = outer_rows(g_head, v_head)
        delta = jnp.sum(shares * d_shares, axis=1, keepdims=True)
        d_scores = (shares * (d_shares - delta)).astype(jnp.bfloat16)
        d_query = jnp.dot(d_scores, k_head, preferred_element_type=jnp.float32) * scale
        d_key = inner_rows(d_scores, q_head) * scale
        d_value = inner_rows(shares.astype(jnp.bfloat16), g_head)
        return (running, (d_query, delta[:, 0], d_key, d_value))

    unused, results = lax.scan(one_head, 0, jnp.arange(HEADS))
    return results


def shards(
    tokens, segments, w_qkv, w_out, ln1_gain, ln1_bias, ln2_gain, ln2_bias, w_up, w_down, out_grad
):
    width = tokens.shape[1]
    rows = tokens.shape[0]
    scale = 1.0 / math.sqrt(HEAD_DIM)
    qkv_full, out_full, gain_one, bias_one, gain_two, bias_two = (
        lax.all_gather(w_qkv, "shard", axis=0, tiled=True),
        lax.all_gather(w_out, "shard", axis=0, tiled=True),
        lax.all_gather(ln1_gain, "shard", axis=0, tiled=True),
        lax.all_gather(ln1_bias, "shard", axis=0, tiled=True),
        lax.all_gather(ln2_gain, "shard", axis=0, tiled=True),
        lax.all_gather(ln2_bias, "shard", axis=0, tiled=True),
    )
    gain_one = gain_one.astype(jnp.float32)
    bias_one = bias_one.astype(jnp.float32)
    gain_two = gain_two.astype(jnp.float32)
    bias_two = bias_two.astype(jnp.float32)
    inputs = tokens.astype(jnp.float32)
    low_one = layer_norm(inputs, gain_one, bias_one).astype(jnp.bfloat16)
    projected = jnp.dot(low_one, qkv_full, preferred_element_type=jnp.float32).astype(jnp.bfloat16)
    queries = projected[:, :width]
    keys = projected[:, width : 2 * width]
    values = projected[:, 2 * width :]
    seq_row = segments[0]
    query_pos = lax.axis_index(("context", "tensor")) * rows + jnp.arange(rows, dtype=jnp.int32)
    keys_all, values_all, seq_all = (
        lax.all_gather(keys, ("context", "tensor"), axis=0, tiled=True),
        lax.all_gather(values, ("context", "tensor"), axis=0, tiled=True),
        lax.all_gather(seq_row, ("context", "tensor"), axis=0, tiled=True),
    )
    key_pos = jnp.arange(keys_all.shape[0], dtype=jnp.int32)
    allowed = make_mask(query_pos, seq_row, key_pos, seq_all)
    attended, totals = attend_forward(queries, keys_all, values_all, allowed, scale)
    attended_low = attended.astype(jnp.bfloat16)
    resid = inputs + jnp.dot(attended_low, out_full, preferred_element_type=jnp.float32)
    low_two = layer_norm(resid, gain_two, bias_two).astype(jnp.bfloat16)
    up_full, down_full = (
        lax.all_gather(w_up, "shard", axis=0, tiled=True),
        lax.all_gather(w_down, "shard", axis=1, tiled=True),
    )
    rows_all = lax.all_gather(low_two, "tensor", axis=0, tiled=True)
    hidden_pre = jnp.dot(rows_all, up_full, preferred_element_type=jnp.float32)
    hidden_low = jax.nn.gelu(hidden_pre, approximate=True).astype(jnp.bfloat16)
    mixed = lax.psum_scatter(
        jnp.dot(hidden_low, down_full, preferred_element_type=jnp.float32).astype(jnp.bfloat16),
        "tensor",
        scatter_dimension=0,
        tiled=True,
    ).astype(jnp.float32)
    result = (resid + mixed).astype(jnp.bfloat16)
    grad_in = out_grad.astype(jnp.float32)
    grads_all = lax.all_gather(out_grad, "tensor", axis=0, tiled=True)
    d_hidden = outer_rows(grads_all, down_full)
    unused, gelu_pull = jax.vjp(
        lambda values_in: jax.nn.gelu(values_in, approximate=True), hidden_pre
    )
    d_pre = gelu_pull(d_hidden)[0].astype(jnp.bfloat16)
    grad_down = inner_rows(hidden_low, grads_all)
    grad_up = inner_rows(rows_all, d_pre)
    d_normed_two = lax.psum_scatter(
        outer_rows(d_pre, up_full), "tensor", scatter_dimension=0, tiled=True
    )
    unused, second_pull = jax.vjp(layer_norm, resid, gain_two, bias_two)
    d_resid_norm, grad_gain_two, grad_bias_two = second_pull(d_normed_two)
    d_resid = grad_in + d_resid_norm
    d_branch = d_resid.astype(jnp.bfloat16)
    grad_out_w = inner_rows(attended_low, d_branch)
    d_attended = outer_rows(d_branch, out_full).astype(jnp.bfloat16)
    keys_back, values_back, seq_back, allowed_back = (keys_all, values_all, seq_all, allowed)
    d_queries, deltas, d_keys_h, d_values_h = attend_backward(
        queries, keys_back, values_back, allowed_back, d_attended, totals, scale
    )
    d_keys_sum, d_values_sum = (
        lax.psum_scatter(
            join_heads(d_keys_h), ("context", "tensor"), scatter_dimension=0, tiled=True
        ),
        lax.psum_scatter(
            join_heads(d_values_h), ("context", "tensor"), scatter_dimension=0, tiled=True
        ),
    )
    d_keys = d_keys_sum.astype(jnp.bfloat16)
    d_values = d_values_sum.astype(jnp.bfloat16)
    d_projected = jnp.concatenate(
        [join_heads(d_queries).astype(jnp.bfloat16), d_keys, d_values], axis=1
    )
    grad_qkv = inner_rows(low_one, d_projected)
    d_normed_one = outer_rows(d_projected, qkv_full)
    unused, first_pull = jax.vjp(layer_norm, inputs, gain_one, bias_one)
    d_inputs, grad_gain_one, grad_bias_one = first_pull(d_normed_one)
    input_grad = (d_resid + d_inputs).astype(jnp.bfloat16)
    shares_out = (
        lax.psum_scatter(grad_qkv, "shard", scatter_dimension=0, tiled=True),
        lax.psum_scatter(grad_out_w, "shard", scatter_dimension=0, tiled=True),
        lax.psum_scatter(grad_gain_one, "shard", scatter_dimension=0, tiled=True),
        lax.psum_scatter(grad_bias_one, "shard", scatter_dimension=0, tiled=True),
        lax.psum_scatter(grad_gain_two, "shard", scatter_dimension=0, tiled=True),
        lax.psum_scatter(grad_bias_two, "shard", scatter_dimension=0, tiled=True),
        lax.psum_scatter(grad_up, "shard", scatter_dimension=0, tiled=True),
        lax.psum_scatter(grad_down, "shard", scatter_dimension=1, tiled=True),
    )
    attn_sums = lax.psum(
        (shares_out[0], shares_out[1], shares_out[2], shares_out[3], shares_out[4], shares_out[5]),
        ("context", "tensor"),
    )
    mlp_sums = lax.psum((shares_out[6], shares_out[7]), "context")
    return (
        result,
        input_grad,
        attn_sums[0],
        attn_sums[1],
        attn_sums[2],
        attn_sums[3],
        attn_sums[4],
        attn_sums[5],
        mlp_sums[0],
        mlp_sums[1],
    )


def solution(mesh):
    in_specs = (
        P(("shard", "context", "tensor"), None),
        P("shard", ("context", "tensor")),
        P("shard", None),
        P("shard", None),
        P("shard"),
        P("shard"),
        P("shard"),
        P("shard"),
        P("shard", "tensor"),
        P("tensor", "shard"),
        P(("shard", "context", "tensor"), None),
    )
    out_specs = (
        P(("shard", "context", "tensor"), None),
        P(("shard", "context", "tensor"), None),
        P("shard", None),
        P("shard", None),
        P("shard"),
        P("shard"),
        P("shard"),
        P("shard"),
        P("shard", "tensor"),
        P("tensor", "shard"),
    )
    return jax.shard_map(shards, mesh=mesh, in_specs=in_specs, out_specs=out_specs, check_vma=False)
```

profile of v0, /device:TPU:0, one launch (start us, length us, event | category | flops | bytes accessed | tf_op | source)
XLA Modules:
  0.0 1691.4 jit_solution(3931462748428171783)
XLA Ops:
  10.3 9.6 all-reduce.13
  20.3 83.1 %all-gather.10.cloned.1.call-done = bf16[1088,3264]{1,0:T(8,128)(2,1)} async-done(((bf16[544,3264]{1,0:T(8,128)(2,1)}), bf16[1088,3264]{1,0:T(8,128)(2,1)}) %all-gather.10.cloned.1.call-update) | async-done | bytes 7102480 | tf_op jit(solution)/shard_map/all_gather | solution.py:89
  103.4 4.7 convolution_convert_fusion
  114.0 63.8 %all-reduce.2 = s32[2560]{0:T(1024)S(1)} all-reduce(s32[2560]{0:T(1024)S(1)} %dynamic-update-slice.2), channel_id=2, replica_groups=mesh['shard'=2,'context'=4,'tensor'=4] {'context','tensor'}, use_global_device_ids=true, to_apply=%add.2 | all-reduce | flops 2560 | bytes 20480
  177.8 52.5 %all-gather.12.cloned.1.call-done = bf16[2560,1088]{1,0:T(8,128)(2,1)} async-done(((bf16[160,1088]{1,0:T(8,128)(2,1)}), bf16[2560,1088]{1,0:T(8,128)(2,1)}) %all-gather.12.cloned.1.call-update) | async-done | bytes 5570576 | tf_op jit(solution)/shard_map/all_gather | solution.py:109
  230.4 93.5 %while.28 = (s32[]{:T(128)}, bf16[17,160,64]{1,2,0:T(8,128)(2,1)S(1)}, f32[17,160]{1,0:T(8,128)S(1)}, s32[17]{0:T(128)S(1)}, bf16[160,1088]{1,0:T(8,128)(2,1)S(1...) while((s32[]{:T(128)}, ...), condition=%wide.region_5.6_spmd.clone, body=%wide.region_2.5_spmd.clone.sunk | while | flops 108953440 | bytes 6354131 | solution.py:57
  328.7 14.4 all-gather.22.cloned.1.call-done
  343.1 6.0 fusion.71
  349.1 33.3 %all-gather.20.cloned.1.call-done = bf16[1088,1088]{1,0:T(8,128)(2,1)} async-done(((bf16[544,1088]{1,0:T(8,128)(2,1)}), bf16[1088,1088]{1,0:T(8,128)(2,1)}) %all-gather.20.cloned.1.call-update) | async-done | bytes 2367504 | tf_op jit(solution)/shard_map/all_gather | solution.py:120
  382.4 37.5 %all-gather.18.cloned.1.call-done = bf16[640,1088]{1,0:T(8,128)(2,1)} async-done(((bf16[160,1088]{1,0:T(8,128)(2,1)}), bf16[640,1088]{1,0:T(8,128)(2,1)}) %all-gather.18.cloned.1.call-update) | async-done | bytes 1392656 | tf_op jit(solution)/shard_map/all_gather | solution.py:123
  419.9 8.5 fusion.42
  433.5 6.4 convolution_convert_fusion.1
  440.2 49.7 %reduce-scatter.15.cloned.1.call-done = f32[160,1088]{1,0:T(8,128)} async-done(((f32[640,1088]{1,0:T(8,128)}), f32[160,1088]{1,0:T(8,128)}) %reduce-scatter.15.cloned.1.call-update) | async-done | bytes 696336 | tf_op jit(solution)/shard_map/reduce_scatter | solution.py:142
  491.4 35.0 %reduce-scatter.13.cloned.1.call-done = bf16[160,1088]{1,0:T(8,128)(2,1)} async-done(((bf16[640,1088]{1,0:T(8,128)(2,1)}), bf16[160,1088]{1,0:T(8,128)(2,1)}) %reduce-scatter.13.cloned.1.call-update) | async-done | bytes 348176 | tf_op jit(solution)/shard_map/reduce_scatter | solution.py:126
  530.0 207.9 %while.29 = (s32[]{:T(128)}, bf16[17,160,64]{1,2,0:T(8,128)(2,1)S(1)}, f32[17,2560,64]{1,2,0:T(8,128)}, f32[17,2560,64]{1,2,0:T(8,128)}, s32[17]{0:T(128)S(1)}, ...) while((s32[]{:T(128)}, ...), condition=%wide.region_14.15_spmd.clone, body=%wide.region_12.14_spmd.clone.sunk | while | flops 267233120 | bytes 15811237 | solution.py:78
  738.0 13.0 copy.23
  751.1 13.2 copy.21
  764.4 6.9 fusion.74
  771.4 7.3 fusion.64
  782.3 96.6 %reduce-scatter.27.cloned.1.call-done = f32[160,1088]{1,0:T(8,128)} async-done(((f32[2560,1088]{1,0:T(8,128)}), f32[160,1088]{1,0:T(8,128)}) %reduce-scatter.27.cloned.1.call-update) | async-done | bytes 696336
  880.2 130.9 %reduce-scatter.25.cloned.1.call-done = f32[160,1088]{1,0:T(8,128)} async-done(((f32[2560,1088]{1,0:T(8,128)}), f32[160,1088]{1,0:T(8,128)}) %reduce-scatter.25.cloned.1.call-update) | async-done | bytes 696336
  1012.4 8.0 fusion.54
  1020.5 55.5 %reduce-scatter.21.cloned.1.call-done = f32[544,1088]{1,0:T(8,128)} async-done(((f32[1088,1088]{1,0:T(8,128)}), f32[544,1088]{1,0:T(8,128)}) %reduce-scatter.21.cloned.1.call-update) | async-done | bytes 2367504 | tf_op jit(solution)/shard_map/reduce_scatter | solution.py:180
  1076.0 65.5 %reduce-scatter.23.cloned.1.call-done = f32[1088,544]{0,1:T(8,128)} async-done(((f32[1088,1088]{0,1:T(8,128)}), f32[1088,544]{0,1:T(8,128)}) %reduce-scatter.23.cloned.1.call-update) | async-done | bytes 2367504 | tf_op jit(solution)/shard_map/reduce_scatter | solution.py:181
  1141.6 66.0 %reduce-scatter.19.cloned.1.call-done = f32[544,1088]{1,0:T(8,128)} async-done(((f32[1088,1088]{1,0:T(8,128)}), f32[544,1088]{1,0:T(8,128)}) %reduce-scatter.19.cloned.1.call-update) | async-done | bytes 2367504 | tf_op jit(solution)/shard_map/reduce_scatter | solution.py:175
  1207.5 167.2 %reduce-scatter.17.cloned.1.call-done = f32[544,3264]{1,0:T(8,128)} async-done(((f32[1088,3264]{1,0:T(8,128)}), f32[544,3264]{1,0:T(8,128)}) %reduce-scatter.17.cloned.1.call-update) | async-done | bytes 7102480 | tf_op jit(solution)/shard_map/reduce_scatter | solution.py:174
  1375.4 6.1 fusion.65
  1382.0 7.2 all-reduce.12
  1389.6 61.6 %all-reduce.9 = (f32[544]{0:T(1024)}, f32[544]{0:T(1024)}, f32[544]{0:T(1024)}, f32[544]{0:T(1024)}) all-reduce(f32[544]{0:T(1024)S(1)} %dynamic-slice.6, f32[544]{0:T(1024)S(1)} %dynamic-slice.8, f32[544]{0:T(1024)S(1)} %dynamic-slice.10, ...), channel_id=1, replica_groups=mesh['shard'=2,'context'=4,'tensor'=4] {'context','tensor'}, use_global_device_ids=true, to_apply=%region_25.26 | all-reduce | flops 2176 | bytes 17408 | tf_op jit(solution)/shard_map/psum | solution.py:183
  1452.3 24.1 %all-reduce.19.cloned.1.call-done = (f32[544,1088]{1,0:T(8,128)}, f32[1088,544]{0,1:T(8,128)}) async-done(((f32[544,1088]{1,0:T(8,128)}, f32[1088,544]{0,1:T(8,128)}), (f32[544,1088]{1,0:T(8,128)}, f32[1088,544]{0,1:T(8,128)})) %all-reduce.19.cloned.1.call-update) | async-done | bytes 4734992 | tf_op jit(solution)/shard_map/psum | solution.py:187
  1476.4 194.3 %all-reduce.17.cloned.1.call-done = (f32[544,3264]{1,0:T(8,128)}, f32[544,1088]{1,0:T(8,128)}) async-done(((f32[544,3264]{1,0:T(8,128)}, f32[544,1088]{1,0:T(8,128)}), (f32[544,3264]{1,0:T(8,128)}, f32[544,1088]{1,0:T(8,128)})) %all-reduce.17.cloned.1.call-update) | async-done | bytes 9469968 | tf_op jit(solution)/shard_map/psum | solution.py:183
  1670.7 6.7 copy.60
  (368 shorter events, 283.3 us)
Async XLA Ops:
  7.2 2.4 copy-start.11
  7.2 2.6 copy-start.12
  7.2 2.8 copy-start.13
  7.2 12.7 copy-start
  7.2 96.2 %all-gather.10.cloned.1.call-start = ((), (), s32[]{:S(2)}) async-start(), calls=%async_computation.8 | async-start | bytes 10862592 | tf_op jit(solution)/shard_map/all_gather | solution.py:89
  8.0 169.9 %all-gather.14.cloned.1.call-start = ((), (), s32[]{:S(2)}) async-start(), calls=%async_computation.10 | async-start | bytes 6266880 | tf_op jit(solution)/shard_map/all_gather | solution.py:110
  109.1 3.3 copy-start.16
  109.1 4.6 copy-start.14
  109.2 121.1 %all-gather.12.cloned.1.call-start = ((), (), s32[]{:S(2)}) async-start(), calls=%async_computation.9 | async-start | bytes 6266880 | tf_op jit(solution)/shard_map/all_gather | solution.py:109
  109.9 214.0 %all-gather.16.cloned.1.call-start = ((), (), s32[]{:S(2)}) async-start(), calls=%async_computation.11 | async-start | bytes 3760128 | tf_op jit(solution)/shard_map/all_gather | solution.py:90
  110.5 218.2 %all-gather.24.cloned.1.call-start = ((), (), s32[]{:S(2)}) async-start(), calls=%async_computation.16 | async-start | bytes 1843200 | tf_op jit(solution)/shard_map/all_gather | solution.py:134
  111.1 232.0 %all-gather.22.cloned.1.call-start = ((), (), s32[]{:S(2)}) async-start(), calls=%async_computation.14 | async-start | bytes 3760128 | tf_op jit(solution)/shard_map/all_gather | solution.py:121
  111.6 270.7 %all-gather.20.cloned.1.call-start = ((), (), s32[]{:S(2)}) async-start(), calls=%async_computation.13 | async-start | bytes 3760128 | tf_op jit(solution)/shard_map/all_gather | solution.py:120
  112.4 307.5 %all-gather.18.cloned.1.call-start = ((), (), s32[]{:S(2)}) async-start(), calls=%async_computation.12 | async-start | bytes 1843200 | tf_op jit(solution)/shard_map/all_gather | solution.py:123
  328.4 161.5 %reduce-scatter.15.cloned.1.call-start = ((), (), s32[]{:S(2)}) async-start(), calls=%async_computation.17 | async-start | bytes 3686400 | tf_op jit(solution)/shard_map/reduce_scatter | solution.py:142
  419.9 9.6 copy-start.15
  433.5 92.9 %reduce-scatter.13.cloned.1.call-start = ((), (), s32[]{:S(2)}) async-start(), calls=%async_computation.15 | async-start | bytes 1843200 | tf_op jit(solution)/shard_map/reduce_scatter | solution.py:126
  439.9 88.8 %copy-start.2 = (bf16[160,1088]{1,0:T(8,128)(2,1)S(1)}, bf16[160,1088]{1,0:T(8,128)(2,1)}, u32[]{:S(2)}) copy-start(bf16[160,1088]{1,0:T(8,128)(2,1)} %param.25) | copy-start | bytes 1044484
  440.0 438.9 %reduce-scatter.27.cloned.1.call-start = ((), (), s32[]{:S(2)}) async-start(), calls=%async_computation.23 | async-start | bytes 12533760
  526.4 2.6 copy-start.1
  738.0 13.1 copy-start.6
  751.0 260.1 %reduce-scatter.25.cloned.1.call-start = ((), (), s32[]{:S(2)}) async-start(), calls=%async_computation.22 | async-start | bytes 12533760
  764.3 311.7 %reduce-scatter.21.cloned.1.call-start = ((), (), s32[]{:S(2)}) async-start(), calls=%async_computation.20 | async-start | bytes 7520256 | tf_op jit(solution)/shard_map/reduce_scatter | solution.py:180
  771.3 370.1 %reduce-scatter.23.cloned.1.call-start = ((), (), s32[]{:S(2)}) async-start(), calls=%async_computation.21 | async-start | bytes 7520256 | tf_op jit(solution)/shard_map/reduce_scatter | solution.py:181
  778.7 428.8 %reduce-scatter.19.cloned.1.call-start = ((), (), s32[]{:S(2)}) async-start(), calls=%async_computation.19 | async-start | bytes 7520256 | tf_op jit(solution)/shard_map/reduce_scatter | solution.py:175
  781.9 230.5 %copy-start.7 = (bf16[17,160,64]{1,2,0:T(8,128)(2,1)S(1)}, bf16[17,160,64]{1,2,0:T(8,128)(2,1)}, u32[]{:S(2)}) copy-start(bf16[17,160,64]{1,2,0:T(8,128)(2,1)} %copy-done.6) | copy-start | bytes 1044484
  782.0 592.8 %reduce-scatter.17.cloned.1.call-start = ((), (), s32[]{:S(2)}) async-start(), calls=%async_computation.18 | async-start | bytes 21725184 | tf_op jit(solution)/shard_map/reduce_scatter | solution.py:174
  1020.4 456.0 %all-reduce.19.cloned.1.call-start = ((), (), s32[]{:S(2)}) async-start(), calls=%async_computation.25 | async-start | bytes 10027008 | tf_op jit(solution)/shard_map/psum | solution.py:187
  1141.5 529.2 %all-reduce.17.cloned.1.call-start = ((), (), s32[]{:S(2)}) async-start(), calls=%async_computation.24 | async-start | bytes 19496960 | tf_op jit(solution)/shard_map/psum | solution.py:183
  1670.7 6.7 copy-start.5
  1677.4 2.6 copy-start.4
  1680.0 2.6 copy-start.3
  (4 other events, 4.8 us)
Sparse Core Ops, SparseCore 0:
  9.6 93.7 all-gather.9
  109.3 59.9 all-gather.13
  172.2 58.0 all-gather.11
  231.7 36.3 all-gather.15
  269.6 35.2 all-gather.23
  306.3 36.7 all-gather.21
  344.6 37.7 all-gather.19
  384.5 35.3 all-gather.17
  433.6 56.2 reduce-scatter.14
  492.7 33.6 reduce-scatter.12
  751.1 127.6 reduce-scatter.26
  882.8 128.2 reduce-scatter.24
  1013.4 62.5 reduce-scatter.20
  1078.2 63.2 reduce-scatter.22
  1144.2 63.2 reduce-scatter.18
  1209.7 165.0 reduce-scatter.16
  1377.0 99.3 all-reduce.18
  1480.1 190.5 all-reduce.16
where the time goes:
time: 1700 us; the launch traced here: 1690 us
  waiting for transfers between devices  1110 us (65%)
  matrix products  279 us (16%)
  blocking collectives  142 us (8%)
  local copies, waits for them, and re-layouts  68.8 us (4%)
  loops' own time  56.3 us (3%)
  other arithmetic  17.5 us (1%)
  between operations  17 us (1%)
    unnamed x20, waiting for transfers between devices  231 us
    psum x1, waiting for transfers between devices, shards(): lax.psum((shares_out[0], shares_out[1], shares_out[2], shares_out[3], sha...  194 us
    reduce_scatter x1, waiting for transfers between devices, shards(): lax.psum_scatter(grad_qkv, 'shard', scatter_dimension=0, tiled=True)  167 us
    dot_general x55, matrix products, outer_rows(): lax.dot_general(left, right, (((1,), (1,)), ((), ())), preferred_element_...  110 us
    all_gather x1, waiting for transfers between devices, shards(): lax.all_gather(w_qkv, 'shard', axis=0, tiled=True)  83.1 us
    dot_general x38, matrix products, inner_rows(): lax.dot_general(left, right, (((0,), (0,)), ((), ())), preferred_element_...  81.1 us
    unnamed x3, blocking collectives  80.7 us
    reduce_scatter x1, waiting for transfers between devices, shards(): lax.psum_scatter(grad_out_w, 'shard', scatter_dimension=0, tiled=True)  66 us
  transfers between devices with their start and end apart: 18, of which 15 were waited for; matrix products, arithmetic and copies ran while one was open for 9% of the time, Pallas kernels for 0%

commit v1 on v0

v1 whole, which is shorter than its diff:
```python
import functools
import math

import jax
import jax.numpy as jnp
from jax import lax
from jax.experimental import pallas as pl
from jax.experimental.pallas import tpu as pltpu
from jax.sharding import PartitionSpec as P

HEADS = 17
HEAD_DIM = 64
SEQS = 6
EPSILON = 1e-05
NEG = -1e30
GROUP = ("context", "tensor")
TILE = 256
BF = jnp.bfloat16
F32 = jnp.float32


def contract(left, right, left_dim, right_dim):
    return lax.dot_general(
        left, right, (((left_dim,), (right_dim,)), ((), ())), preferred_element_type=F32
    )


def norm_stats(values):
    average = jnp.mean(values, axis=-1, keepdims=True)
    centred = values - average
    variance = jnp.mean(centred * centred, axis=-1, keepdims=True)
    inverse = lax.rsqrt(variance + EPSILON)
    return centred * inverse, inverse


def norm_back(grad, unit, inverse, gain):
    scaled = grad * gain
    first = jnp.mean(scaled, axis=-1, keepdims=True)
    second = jnp.mean(scaled * unit, axis=-1, keepdims=True)
    return inverse * (scaled - first - unit * second)


def swap_shard(part):
    return lax.ppermute(part, "shard", [(0, 1), (1, 0)])


def in_order(mine, other, axis):
    index = lax.axis_index("shard")
    return jnp.where(
        index == 0,
        jnp.concatenate([mine, other], axis=axis),
        jnp.concatenate([other, mine], axis=axis),
    )


def gather_small(part, count, axis):
    if count != 2:
        return lax.all_gather(part, "shard", axis=axis, tiled=True)
    return in_order(part, swap_shard(part), axis)


def gather_large(part, count, axis):
    if count != 2:
        return lax.all_gather(part, "shard", axis=axis, tiled=True)
    ways = lax.axis_size("context")
    core = lax.rem(lax.axis_index("context"), 2)
    half = part.shape[axis] // 2
    mine = lax.dynamic_slice_in_dim(part, core * half, half, axis)
    fetched = swap_shard(mine)
    partner = lax.ppermute(fetched, "context", [(i, i ^ 1) for i in range(ways)])
    other = jnp.where(
        core == 0,
        jnp.concatenate([fetched, partner], axis=axis),
        jnp.concatenate([partner, fetched], axis=axis),
    )
    return in_order(part, other, axis)


def sum_shard_rows(partial, count):
    if count != 2:
        return lax.psum_scatter(
            partial.astype(BF), "shard", scatter_dimension=0, tiled=True
        ).astype(F32)
    rows = partial.shape[0] // 2
    index = lax.axis_index("shard")
    away = lax.dynamic_slice_in_dim(partial, (1 - index) * rows, rows, 0).astype(BF)
    kept = lax.dynamic_slice_in_dim(partial, index * rows, rows, 0)
    return kept + swap_shard(away).astype(F32)


def pick_half(pair, high, scale=1.0):
    first = lax.broadcasted_iota(jnp.int32, pair.shape, 1) < HEAD_DIM
    values = pair.astype(F32) * scale
    return (jnp.where(first, 0.0, values) if high else jnp.where(first, values, 0.0)).astype(BF)


def lane_ids(count):
    return lax.broadcasted_iota(jnp.int32, (1, count), 1)


def band(shape, low, high, first_key):
    key = first_key + lax.broadcasted_iota(jnp.int32, shape, 0)
    return (key >= low) & (key <= high)


def forward_kernel(
    own, seq_own, nat, tr, packed, out_nat, lse, out_last, lse_last, start, start_own, end_own, meta,
    q_pad,
):
    rows = nat.shape[0]
    blocks = rows // TILE
    width = out_last.shape[0]
    scale = 1.0 / math.sqrt(HEAD_DIM)

    seq = tr[256:272, :].astype(F32)[0:1, :]
    mine = seq_own[...]
    begin = jnp.zeros_like(seq)
    begin_own = jnp.zeros_like(mine)
    finish_own = jnp.full_like(mine, float(rows))
    for number in range(1, SEQS):
        before = jnp.sum((seq < number).astype(F32), axis=1, keepdims=True)
        begin = jnp.where(seq >= number, before, begin)
        begin_own = jnp.where(mine >= number, before, begin_own)
        finish_own = jnp.where(mine == number - 1, before, finish_own)
    start[...] = begin.astype(jnp.int32)
    start_own[...] = begin_own.astype(jnp.int32)
    end_own[...] = finish_own.astype(jnp.int32)
    base = pl.multiple_of(own[0], 16)
    meta[2 * blocks] = jnp.min(begin_own).astype(jnp.int32) // TILE
    meta[2 * blocks + 1] = (base + width - 1) // TILE + 1
    meta[2 * blocks + 2] = base // width
    meta[2 * blocks + 3] = (jnp.max(finish_own).astype(jnp.int32) + width - 1) // width

    def scores_of(queries, kb):
        at = pl.multiple_of(kb * TILE, TILE)
        return contract(nat[pl.ds(at, TILE), 128:256], queries, 1, 1), at

    def weigh(shares, v_row, at):
        return contract(tr[v_row : v_row + HEAD_DIM, pl.ds(at, TILE)], shares.astype(BF), 1, 0)

    def step(queries, limits, v_row, kb, carry):
        top, total, acc = carry
        scores, at = scores_of(queries, kb)
        if limits is not None:
            scores = jnp.where(band(scores.shape, *limits, at), scores, NEG)
        now = jnp.maximum(top, jnp.max(scores, axis=0, keepdims=True))
        fade = jnp.exp(top - now)
        shares = jnp.exp(scores - now)
        total = total * fade + jnp.sum(shares, axis=0, keepdims=True)
        return now, total, acc * fade + weigh(shares, v_row, at)

    def one_block(qb, unused):
        at = pl.multiple_of(qb * TILE, TILE)
        queries = pick_half(nat[pl.ds(at, TILE), 0:128], False, scale)
        low = start[:, pl.ds(at, TILE)]
        near = low.astype(F32)
        first = jnp.min(near).astype(jnp.int32) // TILE
        full = jnp.minimum((jnp.max(near).astype(jnp.int32) + TILE - 1) // TILE, qb)
        meta[qb] = first
        meta[blocks + qb] = full
        limits = (low, at + lane_ids(TILE))
        scores, at_key = scores_of(queries, qb)
        scores = jnp.where(band(scores.shape, *limits, at_key), scores, NEG)
        top = jnp.max(scores, axis=0, keepdims=True)
        shares = jnp.exp(scores - top)
        carry = (top, jnp.sum(shares, axis=0, keepdims=True), weigh(shares, 128, at_key))
        carry = lax.fori_loop(first, full, functools.partial(step, queries, limits, 128), carry)
        carry = lax.fori_loop(full, qb, functools.partial(step, queries, None, 128), carry)
        top, total, acc = carry
        lse[:, pl.ds(at, TILE)] = top + jnp.log(total)
        out_nat[pl.ds(at, TILE), :] = (acc / total).T
        return unused

    lax.fori_loop(0, blocks, one_block, 0)

    q_pad[...] = jnp.zeros_like(q_pad)
    q_pad[0:width, :] = pick_half(nat[pl.ds(base, width), 0:128], True, scale)
    limits = (start_own[...], base + lane_ids(TILE))
    carry = (
        jnp.full((1, TILE), NEG, F32),
        jnp.zeros((1, TILE), F32),
        jnp.zeros((HEAD_DIM, TILE), F32),
    )
    top, total, acc = lax.fori_loop(
        meta[2 * blocks],
        meta[2 * blocks + 1],
        functools.partial(step, q_pad[...], limits, 192),
        carry,
    )
    lse_last[...] = top + jnp.log(total)
    out_last[...] = (acc / total).T[0:width, :]

    half = width // 2
    for dest in range(rows // width):
        first = out_nat[dest * width : dest * width + half, :]
        second = out_nat[dest * width + half : (dest + 1) * width, :]
        packed[dest] = jnp.concatenate([first, second], axis=1).astype(BF)


def backward_last_kernel(
    own, meta, start_own, end_own, nat, tr, came, lse_own, delta_own, last_qk, last_v,
    q_rows, o_rows, pad_q, pad_o,
):
    rows = nat.shape[0]
    blocks = rows // TILE
    width = last_qk.shape[0]
    scale = 1.0 / math.sqrt(HEAD_DIM)
    base = pl.multiple_of(own[0], 16)

    q_rows[0:rows, :] = (nat[:, 0:128].astype(F32) * scale).astype(BF)
    q_rows[rows:, :] = jnp.zeros((q_rows.shape[0] - rows, 2 * HEAD_DIM), BF)
    for source in range(rows // width):
        o_rows[source * width : (source + 1) * width, :] = came[source, 0:width, :]
    o_rows[rows:, :] = jnp.zeros((o_rows.shape[0] - rows, 2 * HEAD_DIM), BF)

    pad_q[...] = jnp.zeros_like(pad_q)
    pad_o[...] = jnp.zeros_like(pad_o)
    pad_q[0:width, :] = pick_half(nat[pl.ds(base, width), 0:128], True, scale)
    pad_o[0:width, :] = pick_half(o_rows[pl.ds(base, width), :], True)
    limits = (start_own[...], base + lane_ids(TILE))

    def query_step(kb, d_query):
        at = pl.multiple_of(kb * TILE, TILE)
        scores = contract(nat[pl.ds(at, TILE), 128:256], pad_q[...], 1, 1)
        scores = jnp.where(band(scores.shape, *limits, at), scores, NEG)
        shares = jnp.exp(scores - lse_own[...])
        d_shares = contract(nat[pl.ds(at, TILE), 256:384], pad_o[...], 1, 1)
        d_scores = (shares * (d_shares - delta_own[...])).astype(BF)
        return d_query + contract(tr[HEAD_DIM : 2 * HEAD_DIM, pl.ds(at, TILE)], d_scores, 1, 0)

    d_query = lax.fori_loop(
        meta[2 * blocks], meta[2 * blocks + 1], query_step, jnp.zeros((HEAD_DIM, TILE), F32)
    )
    last_qk[:, 0:HEAD_DIM] = (d_query.T[0:width, :] * scale).astype(BF)

    keys = pick_half(nat[pl.ds(base, width), 128:256], True)
    values = pick_half(nat[pl.ds(base, width), 256:384], True)
    key = base + lax.broadcasted_iota(jnp.int32, (width, TILE), 0)
    finish = jnp.broadcast_to(end_own[...].astype(F32), (128, TILE)).T[0:width, 0:1]
    finish = finish.astype(jnp.int32)
    lane = lane_ids(TILE)

    def key_step(source, carry):
        d_key, d_value = carry
        at = pl.multiple_of(source * width, 16)
        queries = q_rows[pl.ds(at, TILE), :]
        grads = o_rows[pl.ds(at, TILE), :]
        facts = came[source, width : width + 16, :].astype(F32)
        log_total = jnp.concatenate([facts[0:1] + facts[2:3], facts[1:2] + facts[3:4]], axis=1)
        delta = jnp.concatenate([facts[4:5] + facts[6:7], facts[5:6] + facts[7:8]], axis=1)
        query = at + lane
        keep = (key <= query) & (query < finish) & (lane < width)
        scores = jnp.where(keep, contract(keys, queries, 1, 1), NEG)
        shares = jnp.exp(scores - log_total)
        d_shares = contract(values, grads, 1, 1)
        d_scores = (shares * (d_shares - delta)).astype(BF)
        return (
            d_key + contract(d_scores, queries, 1, 0),
            d_value + contract(shares.astype(BF), grads, 1, 0),
        )

    zero = jnp.zeros((width, 2 * HEAD_DIM), F32)
    d_key, d_value = lax.fori_loop(
        meta[2 * blocks + 2], meta[2 * blocks + 3], key_step, (zero, zero)
    )
    last_qk[:, HEAD_DIM:] = d_key[:, HEAD_DIM:].astype(BF)
    last_v[...] = d_value[:, HEAD_DIM:].astype(BF)


def backward_kernel(
    meta, start, nat, tr, came, out_nat, lse, packed, d_qk, d_v, o_rows, q_rows, acc_k, acc_v
):
    rows = nat.shape[0]
    blocks = rows // TILE
    width = rows // packed.shape[0]
    scale = 1.0 / math.sqrt(HEAD_DIM)

    q_rows[...] = (nat[:, 0:128].astype(F32) * scale).astype(BF)
    for source in range(rows // width):
        o_rows[source * width : (source + 1) * width, :] = came[source, 0:width, :]
    acc_k[...] = jnp.zeros_like(acc_k)
    acc_v[...] = jnp.zeros_like(acc_v)

    def one_block(qb, unused):
        at_q = pl.multiple_of(qb * TILE, TILE)
        pair = q_rows[pl.ds(at_q, TILE), :]
        queries = pick_half(pair, False)
        grads = o_rows[pl.ds(at_q, TILE), :]
        product = grads[:, 0:HEAD_DIM].astype(F32) * out_nat[pl.ds(at_q, TILE), :]
        delta = jnp.sum(product.T, axis=0, keepdims=True)
        grads_low = pick_half(grads, False)
        log_total = lse[:, pl.ds(at_q, TILE)]
        limits = (start[:, pl.ds(at_q, TILE)], at_q + lane_ids(TILE))

        def step(masked, kb, d_query):
            at = pl.multiple_of(kb * TILE, TILE)
            scores = contract(nat[pl.ds(at, TILE), 128:256], queries, 1, 1)
            if masked:
                scores = jnp.where(band(scores.shape, *limits, at), scores, NEG)
            shares = jnp.exp(scores - log_total)
            d_shares = contract(nat[pl.ds(at, TILE), 256:384], grads_low, 1, 1)
            d_scores = (shares * (d_shares - delta)).astype(BF)
            acc_v[pl.ds(at, TILE), :] += contract(shares.astype(BF), grads, 1, 0)
            acc_k[pl.ds(at, TILE), :] += contract(d_scores, pair, 1, 0)
            return d_query + contract(tr[0:HEAD_DIM, pl.ds(at, TILE)], d_scores, 1, 0)

        d_query = step(True, qb, jnp.zeros((HEAD_DIM, TILE), F32))
        full = meta[blocks + qb]
        d_query = lax.fori_loop(meta[qb], full, functools.partial(step, True), d_query)
        d_query = lax.fori_loop(full, qb, functools.partial(step, False), d_query)
        d_qk[pl.ds(at_q, TILE), 0:HEAD_DIM] = (d_query.T * scale).astype(BF)
        return unused

    lax.fori_loop(0, blocks, one_block, 0)
    d_qk[:, HEAD_DIM:] = acc_k[:, 0:HEAD_DIM].astype(BF)
    d_v[...] = acc_v[:, 0:HEAD_DIM].astype(BF)
    half = width // 2
    for dest in range(rows // width):
        low_rows = slice(dest * width, dest * width + half)
        high_rows = slice(dest * width + half, (dest + 1) * width)
        packed[dest, 0:width, :] = d_qk[dest * width : (dest + 1) * width, :]
        packed[dest, width:, :] = jnp.concatenate([d_v[low_rows, :], d_v[high_rows, :]], axis=1)


def kernel_call(kernel, scalars, operands, outs, scratch, work, smem_out=None):
    vmem = pl.BlockSpec(memory_space=pltpu.VMEM)
    smem = pl.BlockSpec(memory_space=pltpu.SMEM)
    out_shape = [jax.ShapeDtypeStruct(shape, kind) for shape, kind in outs]
    out_specs = [vmem] * len(outs)
    if smem_out is not None:
        out_shape.append(jax.ShapeDtypeStruct((smem_out,), jnp.int32))
        out_specs.append(smem)
    return pl.pallas_call(
        kernel,
        out_shape=tuple(out_shape),
        in_specs=[smem] * len(scalars) + [vmem] * len(operands),
        out_specs=tuple(out_specs),
        scratch_shapes=[pltpu.VMEM(shape, kind) for shape, kind in scratch],
        cost_estimate=pl.CostEstimate(flops=work, bytes_accessed=8 << 20, transcendentals=0),
    )(*scalars, *operands)


def attend_forward(own, seq_own, nat, tr, width):
    rows = nat.shape[0]
    pair = 2 * HEAD_DIM
    return kernel_call(
        forward_kernel,
        (own,),
        (seq_own, nat, tr),
        [
            ((rows // width, width // 2, pair), BF),
            ((rows, HEAD_DIM), F32),
            ((1, rows), F32),
            ((width, HEAD_DIM), F32),
            ((1, TILE), F32),
            ((1, rows), jnp.int32),
            ((1, TILE), jnp.int32),
            ((1, TILE), jnp.int32),
        ],
        [((TILE, pair), BF)],
        16 * rows * rows * HEAD_DIM,
        2 * (rows // TILE) + 4,
    )


def attend_backward_last(own, meta, start_own, end_own, nat, tr, came, lse_own, delta_own, width):
    rows = nat.shape[0]
    pair = 2 * HEAD_DIM
    return kernel_call(
        backward_last_kernel,
        (own, meta),
        (start_own, end_own, nat, tr, came, lse_own, delta_own),
        [((width, pair), BF), ((width, HEAD_DIM), BF)],
        [((rows + TILE - width, pair), BF)] * 2 + [((TILE, pair), BF)] * 2,
        4 * rows * rows * HEAD_DIM,
    )


def attend_backward(meta, start, nat, tr, came, out_nat, lse, width):
    rows = nat.shape[0]
    pair = 2 * HEAD_DIM
    return kernel_call(
        backward_kernel,
        (meta,),
        (start, nat, tr, came, out_nat, lse),
        [
            ((rows // width, width + width // 2, pair), BF),
            ((rows, pair), BF),
            ((rows, HEAD_DIM), BF),
        ],
        [((rows, pair), BF)] * 2 + [((rows, pair), F32)] * 2,
        40 * rows * rows * HEAD_DIM,
    )


def join_kernel(pieces, shared, weights, joined, dots):
    heads = pieces.shape[0]
    total = jnp.zeros((joined.shape[0], 2 * HEAD_DIM), F32)
    rest = 0.0
    units = 3 * (heads + 1)

    def unit(index):
        part, head = divmod(index, heads + 1)
        columns = slice(part * HEAD_DIM, (part + 1) * HEAD_DIM)
        return shared[:, columns] if head == heads else pieces[head, :, columns]

    for block in range((units + 1) // 2):
        paired = 2 * block + 1 < units
        if paired:
            values = jnp.concatenate([unit(2 * block), unit(2 * block + 1)], axis=1)
        else:
            values = unit(2 * block)
        at = slice(2 * block * HEAD_DIM, 2 * block * HEAD_DIM + values.shape[1])
        values = values.astype(F32)
        joined[:, at] = values
        values = values * weights[:, at].astype(F32)
        if paired:
            total = total + values
        else:
            rest = jnp.sum(values, axis=1, keepdims=True)
    dots[...] = jnp.sum(total, axis=1, keepdims=True) + rest


def join_heads(pieces, shared, weights):
    heads, _, columns = pieces.shape
    rows = weights.shape[0]
    step = 272 if rows % 272 == 0 else rows
    return pl.pallas_call(
        join_kernel,
        grid=(rows // step,),
        out_shape=(
            jax.ShapeDtypeStruct(weights.shape, F32),
            jax.ShapeDtypeStruct((rows, 1), F32),
        ),
        in_specs=[
            pl.BlockSpec((heads, step, columns), lambda i: (0, i, 0)),
            pl.BlockSpec((step, shared.shape[1]), lambda i: (i, 0)),
            pl.BlockSpec((step, weights.shape[1]), lambda i: (i, 0)),
        ],
        out_specs=(
            pl.BlockSpec((step, weights.shape[1]), lambda i: (i, 0)),
            pl.BlockSpec((step, 1), lambda i: (i, 0)),
        ),
        cost_estimate=pl.CostEstimate(flops=1 << 20, bytes_accessed=14 << 20, transcendentals=0),
        name="join_heads",
    )(pieces, shared, weights)


def split_two(values):
    high = values.astype(BF)
    low = (values - high.astype(F32)).astype(BF)
    return [high, low]


def round_up(value, step):
    return (value + step - 1) // step * step


def to_tensor(part, ways):
    spread = jnp.broadcast_to(part[None], (ways,) + part.shape)
    got = lax.all_to_all(spread, "tensor", 0, 0, tiled=True)
    return got.reshape(ways * part.shape[0], part.shape[1])


def sum_tensor(partial, ways):
    rows = partial.shape[0] // ways
    got = lax.all_to_all(
        partial.astype(BF).reshape(ways, rows, partial.shape[1]), "tensor", 0, 0, tiled=True
    )
    return jnp.sum(got.astype(F32), axis=0)


def head_columns(matrix, head, width):
    return [
        lax.dynamic_slice_in_dim(matrix, part * width + head * HEAD_DIM, HEAD_DIM, 1)
        for part in range(3)
    ]


def gelu_pair(pre):
    factor = math.sqrt(2.0 / math.pi)
    square = pre * pre
    bend = jnp.tanh(factor * (pre + 0.044715 * pre * square))
    value = 0.5 * pre * (1.0 + bend)
    slope = 0.5 * (1.0 + bend) + 0.5 * pre * (1.0 - bend * bend) * factor * (
        1.0 + 3.0 * 0.044715 * square
    )
    return value, slope


def after(value, *others):
    return lax.optimization_barrier((value,) + others)[0]


def shards(
    tokens, segments, w_qkv, w_out, ln1_gain, ln1_bias, ln2_gain, ln2_bias, w_up, w_down, out_grad
):
    rows, width = tokens.shape
    count = lax.axis_size("shard")
    ways_c = lax.axis_size("context")
    ways_t = lax.axis_size("tensor")
    ways = ways_c * ways_t
    part_rows = w_qkv.shape[0]
    device = lax.axis_index(GROUP)
    shared = HEADS - 1
    padded = round_up(width, 128)
    columns = 3 * HEAD_DIM

    vectors = gather_small(
        jnp.stack([ln1_gain, ln1_bias, ln2_gain, ln2_bias]), count, 1
    ).astype(F32)
    gain_one, bias_one, gain_two, bias_two = [vectors[i : i + 1] for i in range(4)]

    inputs = tokens.astype(F32)
    unit_one, inverse_one = norm_stats(inputs)
    low_one = (unit_one * gain_one + bias_one).astype(BF)
    seq_row = segments[0]
    wide_one = jnp.concatenate(
        [low_one, seq_row[:, None].astype(BF), jnp.zeros((rows, padded - width - 1), BF)], axis=1
    )
    rows_one = lax.all_gather(wide_one, GROUP, axis=0, tiled=True)

    mine = head_columns(w_qkv, device, width)
    last = [
        w_qkv[:, part * width + shared * HEAD_DIM : part * width + (shared + 1) * HEAD_DIM]
        for part in range(3)
    ]
    head_w = gather_small(
        jnp.concatenate([mine[0], last[0], mine[1], last[1], mine[2], last[2]], axis=1),
        count,
        0,
    )
    head_w = jnp.pad(head_w, ((0, padded - width), (0, 0)))
    mark = (jnp.arange(padded)[:, None] == width) & (jnp.arange(16)[None] == 0)
    turn_w = jnp.concatenate([head_w[:, 2 * HEAD_DIM :], mark.astype(BF)], axis=1)
    out_full = gather_large(w_out, count, 0)
    up_full = gather_large(w_up, count, 0)
    down_full = gather_large(w_down, count, 1)
    qkv_full = gather_large(w_qkv, count, 0)
    grads_all = lax.all_gather(out_grad, "tensor", axis=0, tiled=True)
    split = ways * HEAD_DIM
    out_wide = jnp.concatenate(
        [
            out_full[:split].reshape(ways, HEAD_DIM, width),
            jnp.broadcast_to(out_full[None, split:], (ways, HEAD_DIM, width)),
        ],
        axis=1,
    ).reshape(2 * split, width)

    own = (device * rows).reshape(1).astype(jnp.int32)
    seq_own = jnp.concatenate(
        [seq_row, jnp.broadcast_to(seq_row[-1:], (TILE - rows,))]
    ).astype(F32)[None]
    nat = jnp.dot(rows_one, head_w, preferred_element_type=F32).astype(BF)
    tr = contract(turn_w, rows_one, 0, 1).astype(BF)
    packed, out_nat, lse, last_out, last_lse, start, start_own, end_own, meta = attend_forward(
        own, seq_own, nat, tr, rows
    )
    got = lax.all_to_all(packed, GROUP, 0, 0, tiled=True)
    half = rows // 2
    got = got.reshape(ways, half, 2, HEAD_DIM).transpose(2, 1, 0, 3).reshape(rows, split)
    attended = jnp.concatenate([got, last_out.astype(BF)], axis=1)

    resid = inputs + jnp.dot(attended, out_full, preferred_element_type=F32)
    unit_two, inverse_two = norm_stats(resid)
    low_two = (unit_two * gain_two + bias_two).astype(BF)

    d_hidden = contract(grads_all, down_full, 1, 1)
    rows_two = to_tensor(low_two, ways_t)
    hidden, slope = gelu_pair(jnp.dot(rows_two, up_full, preferred_element_type=F32))
    hidden = hidden.astype(BF)
    d_pre = (d_hidden * slope).astype(BF)
    d_normed_two = sum_tensor(contract(d_pre, up_full, 1, 1), ways_t)

    grad_up = contract(rows_two, d_pre, 0, 0).astype(BF)
    grad_down = contract(grads_all, hidden, 0, 0).astype(BF)
    pair = lax.psum_scatter(
        jnp.concatenate([grad_up, grad_down], axis=1),
        ("shard", "context"),
        scatter_dimension=0,
        tiled=True,
    )
    mixed = jnp.dot(hidden, down_full, preferred_element_type=F32).astype(BF)
    mixed = sum_tensor(after(mixed, d_normed_two), ways_t)
    result = (resid + mixed).astype(BF)

    grad_in = out_grad.astype(F32)
    d_resid = grad_in + norm_back(d_normed_two, unit_two, inverse_two, gain_two)
    d_branch = d_resid.astype(BF)

    d_wide = contract(d_branch, out_wide, 1, 1).astype(BF)
    last_grad = d_wide[:, HEAD_DIM : 2 * HEAD_DIM]
    last_delta = jnp.sum(last_grad.astype(F32) * last_out, axis=1)
    pieces = split_two(last_lse[0, :rows]) + split_two(last_delta)
    extra = jnp.pad(jnp.stack(pieces), ((0, 0), (0, TILE - rows))).reshape(8, 128)
    extra = jnp.pad(extra, ((0, 8), (0, 0)))
    payload = jnp.concatenate(
        [
            d_wide.reshape(rows, ways, 2 * HEAD_DIM).transpose(1, 0, 2),
            jnp.broadcast_to(extra[None], (ways,) + extra.shape),
        ],
        axis=1,
    )
    came = lax.all_to_all(payload, GROUP, 0, 0, tiled=True)
    delta_own = jnp.pad(last_delta, (0, TILE - rows))[None]

    grad_out_w = jnp.concatenate(
        [
            contract(attended, d_branch, 0, 0).astype(BF),
            jnp.sum(d_normed_two * unit_two, axis=0)[:, None].astype(BF),
            jnp.sum(d_normed_two, axis=0)[:, None].astype(BF),
            jnp.zeros((width, padded - width - 2), BF),
        ],
        axis=1,
    )
    grad_out_w = lax.psum_scatter(grad_out_w, ("shard", "context"), scatter_dimension=0, tiled=True)

    last_qk, last_v = attend_backward_last(
        own, meta, start_own, end_own, nat, tr, came, last_lse, delta_own, rows
    )
    last_all = jnp.concatenate([last_qk, last_v], axis=1)
    grad_last = sum_shard_rows(contract(low_one, last_all, 0, 0), count)
    chunk = round_up(-(-part_rows // ways), 16)
    grad_last = jnp.pad(grad_last.astype(BF), ((0, chunk * ways - part_rows), (0, 0)))
    grad_last = lax.all_to_all(
        grad_last.reshape(ways, chunk, columns), GROUP, 0, 0, tiled=True
    )
    grad_last = jnp.sum(grad_last.astype(F32), axis=0).astype(BF)

    packed, d_qk, d_v = attend_backward(meta, start, nat, tr, came, out_nat, lse, rows)
    came = lax.all_to_all(packed, GROUP, 0, 0, tiled=True)

    d_head = jnp.concatenate([d_qk, d_v], axis=1)
    grad_mine = contract(rows_one, d_head, 0, 0)[:width]
    sums = jnp.sum(d_head.astype(F32), axis=0).reshape(columns // 2, 2)
    sums_last = jnp.sum(last_all.astype(F32), axis=0).reshape(columns // 2, 2)
    sums = jnp.pad(
        jnp.concatenate([sums, sums_last], axis=1), ((0, part_rows - columns // 2), (0, 0))
    )
    away = jnp.concatenate([jnp.concatenate([grad_mine[i * part_rows : (i + 1) * part_rows], sums], axis=1) for i in range(count)], axis=0)
    both = sum_shard_rows(away, count)
    payload = jnp.concatenate(
        [both.astype(BF), jnp.pad(grad_last, ((0, 0), (0, 4)))], axis=0
    )
    pieces = lax.all_gather(payload, GROUP, axis=0, tiled=False)
    pieces = pieces.reshape(ways, part_rows + chunk, columns + 4)
    shared_w = pieces[:, part_rows:, :columns].reshape(ways * chunk, columns)[:part_rows]
    grad_qkv, dots = join_heads(pieces, shared_w, w_qkv)
    facts = pieces[:, : columns // 2, columns:].astype(F32)
    sums = facts[:, :, :2].reshape(ways, 3, HEAD_DIM)
    sums_last = jnp.sum(facts[:, :, 2:], axis=0).reshape(1, 3, HEAD_DIM)
    sums = jnp.concatenate([sums, sums_last], axis=0).transpose(1, 0, 2).reshape(1, 3 * width)
    grad_bias_one = jnp.sum(w_qkv.astype(F32) * sums, axis=1)
    grad_gain_one = (dots[:, 0] - ln1_bias.astype(F32) * grad_bias_one) / ln1_gain.astype(F32)

    pair = lax.all_gather(pair, "context", axis=0, tiled=True).astype(F32)
    grad_up = pair[:, : up_full.shape[1]]
    grad_down = pair[:, up_full.shape[1] :].T

    piece = part_rows // ways_c
    chunk = round_up(-(-piece // ways_t), 16)
    grad_out_w = jnp.pad(grad_out_w, ((0, chunk * ways_t - piece), (0, 0)))
    grad_out_w = lax.all_to_all(
        grad_out_w.reshape(ways_t, chunk, padded), "tensor", 0, 0, tiled=True
    )
    grad_out_w = jnp.sum(grad_out_w.astype(F32), axis=0).astype(BF)
    grad_out_w = lax.all_gather(grad_out_w, GROUP, axis=0, tiled=False)
    grad_out_w = grad_out_w.reshape(ways_c, chunk * ways_t, padded)[:, :piece]
    grad_out_w = grad_out_w.reshape(part_rows, padded).astype(F32)

    came_qk = came[:, :rows].reshape(ways, rows, 2, HEAD_DIM).transpose(1, 2, 0, 3)
    came_qk = came_qk.reshape(rows, 2, split)
    came_v = came[:, rows:].reshape(ways, half, 2, HEAD_DIM).transpose(2, 1, 0, 3)
    came_v = came_v.reshape(rows, 1, split)
    came = jnp.concatenate([came_qk, came_v], axis=1)
    d_projected = jnp.concatenate(
        [came, last_all.reshape(rows, 3, HEAD_DIM)], axis=2
    ).reshape(rows, 3 * width)
    d_normed_one = contract(d_projected, qkv_full, 1, 1)
    input_grad = (d_resid + norm_back(d_normed_one, unit_one, inverse_one, gain_one)).astype(BF)
    return (
        result,
        input_grad,
        grad_qkv,
        grad_out_w[:, :width],
        grad_gain_one,
        grad_bias_one,
        grad_out_w[:, width],
        grad_out_w[:, width + 1],
        grad_up,
        grad_down,
    )


def solution(mesh):
    in_specs = (
        P(("shard", "context", "tensor"), None),
        P("shard", ("context", "tensor")),
        P("shard", None),
        P("shard", None),
        P("shard"),
        P("shard"),
        P("shard"),
        P("shard"),
        P("shard", "tensor"),
        P("tensor", "shard"),
        P(("shard", "context", "tensor"), None),
    )
    out_specs = (
        P(("shard", "context", "tensor"), None),
        P(("shard", "context", "tensor"), None),
        P("shard", None),
        P("shard", None),
        P("shard"),
        P("shard"),
        P("shard"),
        P("shard"),
        P("shard", "tensor"),
        P("tensor", "shard"),
    )
    return jax.shard_map(shards, mesh=mesh, in_specs=in_specs, out_specs=out_specs, check_vma=False)
```

time: 1700 us -> 559 us (0.33)
  waiting for transfers between devices: 1110 us -> 232 us
  matrix products: 279 us -> 67.8 us
  blocking collectives: 142 us -> 0 us
  Pallas kernels: 0 us -> 57.1 us
  loops' own time: 56.3 us -> 0 us
  starting transfers between devices: 1.36 us -> 45.3 us
  other arithmetic: 17.5 us -> 48.4 us
    reduce_scatter x6 -> x0, waiting for transfers between devices: 439 us -> none  [the longest x1 167 us: shards(): lax.psum_scatter(grad_qkv, 'shard', scatter_dimension=0, tiled=True)]
    psum x2 -> x0, waiting for transfers between devices: 218 us -> none  [the longest x1 194 us: shards(): lax.psum((shares_out[0], shares_out[1], shares_out[2], shares_out[3], sha...]
    dot_general x131 -> x14, matrix products: 279 us -> 67.8 us  [the longest x10 43.3 us: contract(): lax.dot_general(left, right, (((left_dim,), (right_dim,)), ((), ())), pre...]
    unnamed x20 -> x9, waiting for transfers between devices: 231 us -> 38.9 us
    all_gather x7 -> x4, waiting for transfers between devices: 221 us -> 33.2 us  [the longest x1 33.2 us: shards(): rows_one = lax.all_gather(wide_one, GROUP, axis=0, tiled=True)]
    all_to_all x0 -> x8, waiting for transfers between devices: none -> 108 us  [the longest x2 51.6 us: sum_tensor(): lax.all_to_all(partial.astype(BF).reshape(ways, rows, partial.shape[1]),...]
    unnamed x3 -> x0, blocking collectives: 80.7 us -> none
    psum x1 -> x0, blocking collectives: 61.6 us -> none  [shards(): lax.psum((shares_out[0], shares_out[1], shares_out[2], shares_out[3], sha...]
  transfers between devices with their start and end apart: 18 -> 27, of which waited for: 15 -> 15; matrix products, arithmetic and copies ran while one was open for 9% -> 25% of each run, Pallas kernels for 0% -> 5%
where the time goes in v1:
time: 559 us; the launch traced here: 549 us
  waiting for transfers between devices  232 us (42%)
  local copies, waits for them, and re-layouts  81.8 us (15%)
  matrix products  67.8 us (12%)
  Pallas kernels  57.1 us (10%)
  other arithmetic  48.4 us (9%)
  starting transfers between devices  45.3 us (8%)
  between operations  16.8 us (3%)
    ppermute x8, waiting for transfers between devices, swap_shard(): return lax.ppermute(part, 'shard', [(0, 1), (1, 0)])  51.7 us
    all_to_all x2, waiting for transfers between devices, sum_tensor(): lax.all_to_all(partial.astype(BF).reshape(ways, rows, partial.shape[1]),...  51.6 us
    pallas_call x3, Pallas kernels, kernel_call(): pl.pallas_call(kernel, out_shape=tuple(out_shape), in_specs=[smem] * len(...  51.2 us
    dot_general x10, matrix products, contract(): lax.dot_general(left, right, (((left_dim,), (right_dim,)), ((), ())), pre...  43.3 us
    unnamed x9, waiting for transfers between devices  38.9 us
    all_gather x1, waiting for transfers between devices, shards(): rows_one = lax.all_gather(wide_one, GROUP, axis=0, tiled=True)  33.2 us
    all_to_all x1, waiting for transfers between devices, shards(): came = lax.all_to_all(packed, GROUP, 0, 0, tiled=True)  28.3 us
    all_to_all x1, waiting for transfers between devices, to_tensor(): got = lax.all_to_all(spread, 'tensor', 0, 0, tiled=True)  13.7 us
  transfers between devices with their start and end apart: 27, of which 15 were waited for; matrix products, arithmetic and copies ran while one was open for 25% of the time, Pallas kernels for 5%

profile of v1, /device:TPU:0, one launch (start us, length us, event | category | flops | bytes accessed | tf_op | source)
XLA Modules:
  0.0 549.0 jit_solution(624628415490757346)
XLA Ops:
  24.7 12.1 %collective-permute-done.2 = bf16[272,1088]{1,0:T(8,128)(2,1)S(1)} collective-permute-done((bf16[272,1088]{1,0:T(8,128)(2,1)S(1)}, bf16[272,1088]{1,0:T(8,128)(2,1)S(1)}, u32[]{:S(2)}, u32[]{:S(2)}) %collective-permute-start.2) | collective-permute-done | bytes 591904 | tf_op jit(solution)/shard_map/ppermute | solution.py:44
  37.9 6.3 %collective-permute-done.1 = bf16[544,384]{1,0:T(8,128)(2,1)S(1)} collective-permute-done((bf16[544,384]{1,0:T(8,128)(2,1)S(1)}, bf16[544,384]{1,0:T(8,128)(2,1)S(1)}, u32[]{:S(2)}, u32[]{:S(2)}) %collective-permute-start.1) | collective-permute-done | bytes 417824 | tf_op jit(solution)/shard_map/ppermute | solution.py:44
  46.2 33.2 %all-gather.9.cloned.1.call-done = bf16[2560,1152]{1,0:T(8,128)(2,1)} async-done(((bf16[160,1152]{1,0:T(8,128)(2,1)}), bf16[2560,1152]{1,0:T(8,128)(2,1)}) %all-gather.9.cloned.1.call-update) | async-done | bytes 5898256 | tf_op jit(solution)/shard_map/all_gather | solution.py:521
  79.3 7.5 %convolution_convert_fusion.3.nat = bf16[2560,384]{1,0:T(8,128)(2,1)} fusion(bf16[2560,1152]{1,0:T(8,128)(2,1)} %all-gather.9.cloned.1.call-done, bf16[1088,384]{1,0:T(8,128)(2,1)S(1)} %maximum_select_fusion.11), kind=kOutput, calls=%fused_computation.15 | convolution fusion | flops 2265907200 | bytes 8699904 | tf_op jit(solution)/shard_map/dot_general | solution.py:554
  90.7 21.7 %shard_map.186 = (bf16[16,80,128]{2,1,0:T(8,128)(2,1)}, f32[2560,64]{1,0:T(8,128)}, f32[1,2560]{1,0:T(1,128)}, f32[160,64]{1,0:T(8,128)}, f32[1,256]{1,0:T(1,128...) custom-call(s32[1]{0:T(128)} %bitcast.own, f32[1,256]{1,0:T(1,128)} %bitcast.92, ...), custom_call_target="tpu_custom_call" | custom-call | flops 6710886400 | bytes 8388608 | tf_op jit(solution)/shard_map/pallas_call | solution.py:333
  112.5 6.5 %all-to-all-start = ((bf16[16,80,128]{2,1,0:T(8,128)(2,1)}), bf16[16,80,128]{2,1,0:T(8,128)(2,1)S(1)}, u32[]{:S(2)}, u32[]{:S(2)}) async-start(bf16[16,80,128]{2,1,0:T(8,128)(2,1)} %get-tuple-element.27), calls=%async_computation | async-start | bytes 655360 | tf_op jit(solution)/shard_map/all_to_all | solution.py:559
  122.2 8.1 %all-to-all-done = bf16[16,80,128]{2,1,0:T(8,128)(2,1)S(1)} async-done(((bf16[16,80,128]{2,1,0:T(8,128)(2,1)}), bf16[16,80,128]{2,1,0:T(8,128)(2,1)S(1)}, u32[]{:S(2)}, u32[]{:S(2)}) %all-to-all-start) | async-done | bytes 327712 | tf_op jit(solution)/shard_map/all_to_all | solution.py:559
  137.7 4.4 all-to-all-start.1
  148.1 13.2 %collective-permute-done.6 = bf16[1088,272]{0,1:T(8,128)(2,1)} collective-permute-done((bf16[1088,272]{0,1:T(8,128)(2,1)}, bf16[1088,272]{0,1:T(8,128)(2,1)}, u32[]{:S(2)}, u32[]{:S(2)}) %collective-permute-start.6) | collective-permute-done | bytes 591904 | tf_op jit(solution)/shard_map/ppermute | solution.py:44
  161.3 12.2 %collective-permute-done.4 = bf16[272,1088]{1,0:T(8,128)(2,1)} collective-permute-done((bf16[272,1088]{1,0:T(8,128)(2,1)}, bf16[272,1088]{1,0:T(8,128)(2,1)}, u32[]{:S(2)}, u32[]{:S(2)}) %collective-permute-start.4) | collective-permute-done | bytes 591904 | tf_op jit(solution)/shard_map/ppermute | solution.py:44
  186.0 13.7 %all-to-all-done.1 = bf16[4,160,1088]{2,1,0:T(8,128)(2,1)} async-done(((bf16[4,160,1088]{2,1,0:T(8,128)(2,1)}), bf16[4,160,1088]{2,1,0:T(8,128)(2,1)}, u32[]{:S(2)}, u32[]{:S(2)}) %all-to-all-start.1) | async-done | bytes 1392672 | tf_op jit(solution)/shard_map/all_to_all | solution.py:461
  199.8 6.8 %fusion.29 = f32[640,1088]{0,1:T(8,128)} fusion(bf16[640,1088]{1,0:T(8,128)(2,1)} %bitcast.7, bf16[544,1088]{1,0:T(8,128)(2,1)} %maximum_select_fusion.10, bf16[544,1088]{1,0:T(8,128)(2,1)} %param.19, pred[]{:T(512)S(6)} %eq.33), kind=kOutput, calls=%fused_computation.78 | convolution fusion | flops 1525846016 | bytes 6545409 | tf_op jit(solution)/shard_map/dot_general | solution.py:570
  206.6 7.0 %fusion.9 = bf16[640,1088]{0,1:T(8,128)(2,1)S(1)} fusion(bf16[640,1088]{1,0:T(8,128)(2,1)} %all-gather.11.cloned.1.call-done, f32[640,1088]{0,1:T(8,128)} %fusion.29, bf16[1088,544]{1,0:T(8,128)(2,1)} %maximum_select_fusion.8, bf16[1088,544]{1,0:T(8,128)(2,1)} %copy.121, pred[]{:T(512)S(6)} %eq.33), kind=kOutput, calls=%fused_computation.22 | convolution fusion | flops 1538379776 | bytes 7938049 | tf_op jit(solution)/shard_map/dot_general | solution.py:23
  224.8 6.6 %convolution_convert_fusion.5 = bf16[640,1088]{0,1:T(8,128)(2,1)} fusion(bf16[640,1088]{0,1:T(8,128)(2,1)} %copy-done.35, bf16[544,1088]{1,0:T(8,128)(2,1)} %maximum_select_fusion.10, bf16[544,1088]{1,0:T(8,128)(2,1)} %param.19, pred[]{:T(512)S(6)} %eq.33), kind=kOutput, calls=%fused_computation.20 | convolution fusion | flops 1526542336 | bytes 5152769 | tf_op jit(solution)/shard_map/dot_general | solution.py:23
  235.0 4.5 all-to-all-start.2
  239.5 8.4 %convolution_convert_fusion.6 = bf16[640,1088]{0,1:T(8,128)(2,1)} fusion(bf16[1088,544]{1,0:T(8,128)(2,1)} %maximum_select_fusion.8, bf16[1088,544]{1,0:T(8,128)(2,1)} %copy.121, pred[]{:T(512)S(6)} %eq.33, f32[640,1088]{0,1:T(8,128)} %fusion.29), kind=kOutput, calls=%fused_computation.21 | convolution fusion | flops 1532809216 | bytes 6545409 | tf_op jit(solution)/shard_map/dot_general | solution.py:583
  247.9 22.8 %all-to-all-done.2 = bf16[4,160,1088]{2,1,0:T(8,128)(2,1)} async-done(((bf16[4,160,1088]{2,1,0:T(8,128)(2,1)}), bf16[4,160,1088]{2,1,0:T(8,128)(2,1)}, u32[]{:S(2)}, u32[]{:S(2)}) %all-to-all-start.2) | async-done | bytes 1392672 | tf_op jit(solution)/shard_map/all_to_all | solution.py:467
  276.7 4.3 all-to-all-start.3
  286.7 28.8 %all-to-all-done.3 = bf16[4,160,1088]{2,1,0:T(8,128)(2,1)} async-done(((bf16[4,160,1088]{2,1,0:T(8,128)(2,1)}), bf16[4,160,1088]{2,1,0:T(8,128)(2,1)}, u32[]{:S(2)}, u32[]{:S(2)}) %all-to-all-start.3) | async-done | bytes 1392672 | tf_op jit(solution)/shard_map/all_to_all | solution.py:467
  322.6 5.2 concatenate.153
  332.2 4.3 convolution_convert_fusion.7
  337.9 4.2 all-to-all-start.4
  346.2 38.8 %reduce-scatter.7.cloned.1.call-done = bf16[136,1152]{1,0:T(8,128)(2,1)} async-done(((bf16[1088,1152]{1,0:T(8,128)(2,1)}), bf16[136,1152]{1,0:T(8,128)(2,1)}) %reduce-scatter.7.cloned.1.call-update) | async-done | bytes 313360
  386.7 4.6 all-to-all-start.7
  391.3 7.9 %shard_map.188 = (bf16[160,128]{1,0:T(8,128)(2,1)}, bf16[160,64]{1,0:T(8,128)(2,1)}) custom-call(s32[1]{0:T(128)} %bitcast.own, s32[24]{0:T(128)} %get-tuple-element.30.meta, s32[1,256]{1,0:T(1,128)} %get-tuple-element.36.start_own, s32[1,256]{1,0:T(1,128)} %get-tuple-element.37.end_own, bf16[2560,384]{1,0:T(8,128)(2,1)} %convolution_convert_fusion.3.nat, ...), custom_call_target="tpu_custom_call" | custom-call | flops 1677721600 | bytes 8388608 | tf_op jit(solution)/shard_map/pallas_call | solution.py:333
  404.7 21.5 %shard_map.187 = (bf16[16,240,128]{2,1,0:T(8,128)(2,1)}, bf16[2560,128]{1,0:T(8,128)(2,1)}, bf16[2560,64]{1,0:T(8,128)(2,1)}) custom-call(s32[24]{0:T(128)} %get-tuple-element.30.meta, s32[1,2560]{1,0:T(1,128)} %get-tuple-element.31.start, bf16[2560,384]{1,0:T(8,128)(2,1)} %convolution_convert_fusion.3.nat, bf16[272,2560]{1,0:T(8,128)(2,1)} %convolution_convert_fusion.4.tr, ...), custom_call_target="tpu_custom_call" | custom-call | flops 16777216000 | bytes 8388608 | tf_op jit(solution)/shard_map/pallas_call | solution.py:333
  430.6 4.6 fusion.56
  441.4 7.8 %collective-permute-done.10 = bf16[544,196]{0,1:T(8,128)(2,1)S(1)} collective-permute-done((bf16[544,196]{0,1:T(8,128)(2,1)S(1)}, bf16[544,196]{0,1:T(8,128)(2,1)S(1)}, u32[]{:S(2)}, u32[]{:S(2)}) %collective-permute-start.10) | collective-permute-done | bytes 213280 | tf_op jit(solution)/shard_map/ppermute | solution.py:44
  463.5 28.3 %all-to-all-done.5 = bf16[16,240,128]{2,1,0:T(8,128)(2,1)S(1)} async-done(((bf16[16,240,128]{2,1,0:T(8,128)(2,1)}), bf16[16,240,128]{2,1,0:T(8,128)(2,1)S(1)}, u32[]{:S(2)}, u32[]{:S(2)}) %all-to-all-start.5) | async-done | bytes 983072 | tf_op jit(solution)/shard_map/all_to_all | solution.py:631
  500.2 7.8 %fusion.51 = (f32[160]{0:T(256)S(1)}, f32[160]{0:T(256)S(1)}, f32[160,1088]{1,0:T(8,128)S(1)}) fusion(f32[160]{0:T(256)S(1)} %copy-done.27, f32[160]{0:T(256)S(1)} %copy-done.22, bf16[160,1088]{1,0:T(8,128)(2,1)S(1)} %copy-done.4, f32[1088]{0:T(1024)S(1)} %get-tuple-element.54, bf16[160,3264]{1,0:T(8,128)(2,1)} %reshape.218, ...), kind=kOutput, calls=%fused_computation.145 | convolution fusion | flops 1169573632 | bytes 9198337 | tf_op jit(solution)/shard_map/dot_general | solution.py:23
  526.1 7.5 %copy.138.pieces = bf16[16,592,196]{2,1,0:T(8,128)(2,1)} copy(bf16[16,592,196]{1,2,0:T(8,128)(2,1)} %all-gather.17.cloned.1.call-done) | data formatting | bytes 7426048 | tf_op jit(solution)/shard_map/all_gather | solution.py:645
  533.6 5.9 %join_heads.1 = (f32[544,3264]{1,0:T(8,128)}, f32[544,1]{1,0:T(8,128)}) custom-call(bf16[16,592,196]{2,1,0:T(8,128)(2,1)} %copy.138.pieces, bf16[544,192]{1,0:T(8,128)(2,1)} %slice.128.shared, bf16[544,3264]{1,0:T(8,128)(2,1)} %weights.1), custom_call_target="tpu_custom_call" | custom-call | flops 1048576 | bytes 14680064 | tf_op jit(solution)/shard_map/join_heads/pallas_call | solution.py:428
  (258 shorter events, 155.6 us)
Async XLA Ops:
  8.0 71.3 %all-gather.9.cloned.1.call-start = ((), (), s32[]{:S(2)}) async-start(), calls=%async_computation.10 | async-start | bytes 6266880 | tf_op jit(solution)/shard_map/all_gather | solution.py:521
  10.9 6.3 %collective-permute-start = (bf16[4,544]{1,0:T(4,128)(2,1)S(1)}, bf16[4,544]{1,0:T(4,128)(2,1)S(1)}, u32[]{:S(2)}, u32[]{:S(2)}) collective-permute-start(bf16[4,544]{1,0:T(4,128)(2,1)S(1)} %pad_maximum_fusion.7), channel_id=1, source_target_pairs={{0,16},{16,0},{1,17},{17,1},{2,18},{18,2},{3,19},{19,3},{4,20},{20... | collective-permute-start | bytes 13064 | tf_op jit(solution)/shard_map/ppermute | solution.py:44
  19.7 17.1 %collective-permute-start.2 = (bf16[272,1088]{1,0:T(8,128)(2,1)S(1)}, bf16[272,1088]{1,0:T(8,128)(2,1)S(1)}, u32[]{:S(2)}, u32[]{:S(2)}) collective-permute-start(bf16[272,1088]{1,0:T(8,128)(2,1)S(1)} %constant_dynamic-slice_fusion.3), channel_id=1, source_target_pairs={{0,16},{16,0},{1,17},{17,1},{2,18},{18,2},{3,19},{19,3},{4,20},{20... | collective-permute-start | bytes 1775624 | tf_op jit(solution)/shard_map/ppermute | solution.py:44
  22.0 22.2 %collective-permute-start.1 = (bf16[544,384]{1,0:T(8,128)(2,1)S(1)}, bf16[544,384]{1,0:T(8,128)(2,1)S(1)}, u32[]{:S(2)}, u32[]{:S(2)}) collective-permute-start(bf16[544,384]{1,0:T(8,128)(2,1)S(1)} %concatenate.121), channel_id=1, source_target_pairs={{0,16},{16,0},{1,17},{17,1},{2,18},{18,2},{3,19},{19,3},{4,20},{20... | collective-permute-start | bytes 1253384 | tf_op jit(solution)/shard_map/ppermute | solution.py:44
  36.7 7.9 %collective-permute-start.3 = (bf16[272,1088]{1,0:T(8,128)(2,1)S(1)}, bf16[272,1088]{1,0:T(8,128)(2,1)S(1)}, u32[]{:S(2)}, u32[]{:S(2)}) collective-permute-start(bf16[272,1088]{1,0:T(8,128)(2,1)S(1)} %collective-permute-done.2), channel_id=1, source_target_pairs={{0,4},{4,0},{8,12},{12,8},{1,5},{5,1},{9,13},{13,9},{2,6},{6,2},{1... | collective-permute-start | bytes 1775624 | tf_op jit(solution)/shard_map/ppermute | solution.py:70
  112.5 17.9 %all-to-all-start = ((bf16[16,80,128]{2,1,0:T(8,128)(2,1)}), bf16[16,80,128]{2,1,0:T(8,128)(2,1)S(1)}, u32[]{:S(2)}, u32[]{:S(2)}) async-start(bf16[16,80,128]{2,1,0:T(8,128)(2,1)} %get-tuple-element.27), calls=%async_computation | async-start | bytes 655360 | tf_op jit(solution)/shard_map/all_to_all | solution.py:559
  122.2 205.7 %copy-start = (bf16[1088,1088]{1,0:T(8,128)(2,1)}, bf16[1088,1088]{1,0:T(8,128)(2,1)S(1)}, u32[]{:S(2)}) copy-start(bf16[1088,1088]{1,0:T(8,128)(2,1)S(1)} %maximum_select_fusion.5) | copy-start | bytes 7102468
  136.2 144.9 %copy-start.23 = (f32[160]{0:T(256)}, f32[160]{0:T(256)S(1)}, u32[]{:S(2)}) copy-start(f32[160]{0:T(256)S(1)} %add_rsqrt_fusion) | copy-start | bytes 1924
  137.7 62.1 %all-to-all-start.1 = ((bf16[4,160,1088]{2,1,0:T(8,128)(2,1)}), bf16[4,160,1088]{2,1,0:T(8,128)(2,1)}, u32[]{:S(2)}, u32[]{:S(2)}) async-start(bf16[4,160,1088]{2,1,0:T(8,128)(2,1)} %broadcast_in_dim.19), calls=%async_computation.1 | async-start | bytes 2949120 | tf_op jit(solution)/shard_map/all_to_all | solution.py:461
  142.0 64.6 %all-gather.11.cloned.1.call-start = ((), (), s32[]{:S(2)}) async-start(), calls=%async_computation.11 | async-start | bytes 1843200 | tf_op jit(solution)/shard_map/all_gather | solution.py:540
  144.0 17.3 %collective-permute-start.6 = (bf16[1088,272]{0,1:T(8,128)(2,1)}, bf16[1088,272]{0,1:T(8,128)(2,1)}, u32[]{:S(2)}, u32[]{:S(2)}) collective-permute-start(bf16[1088,272]{0,1:T(8,128)(2,1)} %constant_dynamic-slice_fusion.1), channel_id=1, source_target_pairs={{0,16},{16,0},{1,17},{17,1},{2,18},{18,2},{3,19},{19,3},{4,20},{20... | collective-permute-start | bytes 1775624 | tf_op jit(solution)/shard_map/ppermute | solution.py:44
  147.0 26.6 %collective-permute-start.4 = (bf16[272,1088]{1,0:T(8,128)(2,1)}, bf16[272,1088]{1,0:T(8,128)(2,1)}, u32[]{:S(2)}, u32[]{:S(2)}) collective-permute-start(bf16[272,1088]{1,0:T(8,128)(2,1)} %constant_dynamic-slice_fusion.2), channel_id=1, source_target_pairs={{0,16},{16,0},{1,17},{17,1},{2,18},{18,2},{3,19},{19,3},{4,20},{20... | collective-permute-start | bytes 1775624 | tf_op jit(solution)/shard_map/ppermute | solution.py:44
  148.0 184.1 %reduce-scatter.9.cloned.1.call-start = ((), (), s32[]{:S(2)}) async-start(), calls=%async_computation.16 | async-start | bytes 5326848
  161.3 17.1 %collective-permute-start.7 = (bf16[1088,272]{0,1:T(8,128)(2,1)}, bf16[1088,272]{0,1:T(8,128)(2,1)}, u32[]{:S(2)}, u32[]{:S(2)}) collective-permute-start(bf16[1088,272]{0,1:T(8,128)(2,1)} %collective-permute-done.6), channel_id=1, source_target_pairs={{0,4},{4,0},{8,12},{12,8},{1,5},{5,1},{9,13},{13,9},{2,6},{6,2},{1... | collective-permute-start | bytes 1775624 | tf_op jit(solution)/shard_map/ppermute | solution.py:70
  173.6 7.2 %collective-permute-start.5 = (bf16[272,1088]{1,0:T(8,128)(2,1)}, bf16[272,1088]{1,0:T(8,128)(2,1)}, u32[]{:S(2)}, u32[]{:S(2)}) collective-permute-start(bf16[272,1088]{1,0:T(8,128)(2,1)} %collective-permute-done.4), channel_id=1, source_target_pairs={{0,4},{4,0},{8,12},{12,8},{1,5},{5,1},{9,13},{13,9},{2,6},{6,2},{1... | collective-permute-start | bytes 1775624 | tf_op jit(solution)/shard_map/ppermute | solution.py:70
  235.0 35.7 %all-to-all-start.2 = ((bf16[4,160,1088]{2,1,0:T(8,128)(2,1)}), bf16[4,160,1088]{2,1,0:T(8,128)(2,1)}, u32[]{:S(2)}, u32[]{:S(2)}) async-start(bf16[4,160,1088]{2,1,0:T(8,128)(2,1)} %bitcast.80), calls=%async_computation.2 | async-start | bytes 2949120 | tf_op jit(solution)/shard_map/all_to_all | solution.py:467
  276.7 38.7 %all-to-all-start.3 = ((bf16[4,160,1088]{2,1,0:T(8,128)(2,1)}), bf16[4,160,1088]{2,1,0:T(8,128)(2,1)}, u32[]{:S(2)}, u32[]{:S(2)}) async-start(bf16[4,160,1088]{2,1,0:T(8,128)(2,1)} %bitcast.79), calls=%async_computation.3 | async-start | bytes 2949120 | tf_op jit(solution)/shard_map/all_to_all | solution.py:467
  281.1 103.9 %reduce-scatter.7.cloned.1.call-start = ((), (), s32[]{:S(2)}) async-start(), calls=%async_computation.15 | async-start | bytes 2820096
  283.2 34.0 %copy-start.24 = (f32[160]{0:T(256)S(1)}, f32[160]{0:T(256)}, u32[]{:S(2)}) copy-start(f32[160]{0:T(256)} %copy-done.23) | copy-start | bytes 1924
  327.8 181.3 %all-gather.13.cloned.1.call-start = ((), (), s32[]{:S(2)}) async-start(), calls=%async_computation.12 | async-start | bytes 2959360 | tf_op jit(solution)/shard_map/all_gather | solution.py:656
  337.9 48.9 %all-to-all-start.4 = ((bf16[16,176,128]{2,1,0:T(8,128)(2,1)}), bf16[16,176,128]{2,1,0:T(8,128)(2,1)S(1)}, u32[]{:S(2)}, u32[]{:S(2)}) async-start(bf16[16,176,128]{2,1,0:T(8,128)(2,1)} %pad_maximum_fusion.3), calls=%async_computation.4 | async-start | bytes 1441792 | tf_op jit(solution)/shard_map/all_to_all | solution.py:604
  344.9 109.4 %collective-permute-start.8 = (bf16[272,3264]{1,0:T(8,128)(2,1)}, bf16[272,3264]{1,0:T(8,128)(2,1)}, u32[]{:S(2)}, u32[]{:S(2)}) collective-permute-start(bf16[272,3264]{1,0:T(8,128)(2,1)} %constant_dynamic-slice_fusion), channel_id=1, source_target_pairs={{0,16},{16,0},{1,17},{17,1},{2,18},{18,2},{3,19},{19,3},{4,20},{20... | collective-permute-start | bytes 5326856 | tf_op jit(solution)/shard_map/ppermute | solution.py:44
  386.7 17.3 %all-to-all-start.7 = ((bf16[4,48,1152]{2,1,0:T(8,128)(2,1)}), bf16[4,48,1152]{2,1,0:T(8,128)(2,1)S(1)}, u32[]{:S(2)}, u32[]{:S(2)}) async-start(bf16[4,48,1152]{2,1,0:T(8,128)(2,1)} %bitcast.24), calls=%async_computation.7 | async-start | bytes 884736 | tf_op jit(solution)/shard_map/all_to_all | solution.py:663
  391.3 123.3 %all-gather.15.cloned.1.call-start = ((), (), s32[]{:S(2)}) async-start(), calls=%async_computation.13 | async-start | bytes 1880064 | tf_op jit(solution)/shard_map/all_gather | solution.py:667
  400.9 25.3 %copy-start.15 = (bf16[160,192]{1,0:T(8,128)(2,1)}, bf16[160,192]{1,0:T(8,128)(2,1)S(1)}, u32[]{:S(2)}) copy-start(bf16[160,192]{1,0:T(8,128)(2,1)S(1)} %constant_dynamic-update-slice_fusion) | copy-start | bytes 184324
  401.4 34.2 %collective-permute-start.11 = (bf16[544,192]{0,1:T(8,128)(2,1)S(1)}, bf16[544,192]{0,1:T(8,128)(2,1)S(1)}, u32[]{:S(2)}, u32[]{:S(2)}) collective-permute-start(bf16[544,192]{0,1:T(8,128)(2,1)S(1)} %dynamic-slice_convert_fusion.1), channel_id=1, source_target_pairs={{0,16},{16,0},{1,17},{17,1},{2,18},{18,2},{3,19},{19,3},{4,20},{20... | collective-permute-start | bytes 626696 | tf_op jit(solution)/shard_map/ppermute | solution.py:44
  436.7 16.5 %all-to-all-start.6 = ((bf16[16,48,192]{2,1,0:T(8,128)(2,1)}), bf16[16,48,192]{2,1,0:T(8,128)(2,1)S(1)}, u32[]{:S(2)}, u32[]{:S(2)}) async-start(bf16[16,48,192]{2,1,0:T(8,128)(2,1)} %bitcast.21), calls=%async_computation.6 | async-start | bytes 786432 | tf_op jit(solution)/shard_map/all_to_all | solution.py:625
  440.5 77.2 %all-gather.17.cloned.1.call-start = ((), (), s32[]{:S(2)}) async-start(), calls=%async_computation.14 | async-start | bytes 4352000 | tf_op jit(solution)/shard_map/all_gather | solution.py:645
  440.7 8.6 %collective-permute-start.10 = (bf16[544,196]{0,1:T(8,128)(2,1)S(1)}, bf16[544,196]{0,1:T(8,128)(2,1)S(1)}, u32[]{:S(2)}, u32[]{:S(2)}) collective-permute-start(bf16[544,196]{0,1:T(8,128)(2,1)S(1)} %dynamic-slice_convert_fusion), channel_id=1, source_target_pairs={{0,16},{16,0},{1,17},{17,1},{2,18},{18,2},{3,19},{19,3},{4,20},{20... | collective-permute-start | bytes 639752 | tf_op jit(solution)/shard_map/ppermute | solution.py:44
  454.2 4.0 collective-permute-start.9
  454.3 37.5 %all-to-all-start.5 = ((bf16[16,240,128]{2,1,0:T(8,128)(2,1)}), bf16[16,240,128]{2,1,0:T(8,128)(2,1)S(1)}, u32[]{:S(2)}, u32[]{:S(2)}) async-start(bf16[16,240,128]{2,1,0:T(8,128)(2,1)} %get-tuple-element.35), calls=%async_computation.5 | async-start | bytes 1966080 | tf_op jit(solution)/shard_map/all_to_all | solution.py:631
  526.1 14.5 %copy-start.25 = (f32[544]{0:T(1024)}, f32[544]{0:T(1024)S(1)}, u32[]{:S(2)}) copy-start(f32[544]{0:T(1024)S(1)} %multiply_reduce_fusion) | copy-start | bytes 6532
  (32 other events, 138.4 us)
Sparse Core Ops, SparseCore 0:
  19.7 59.5 all-gather.8
  332.3 31.0 all-gather.12
  404.8 38.6 all-gather.14
  454.4 58.2 all-gather.16
Sparse Core Ops, SparseCore 1:
  148.1 53.0 all-gather.10
  224.9 55.1 reduce-scatter.8
  327.9 57.0 reduce-scatter.6
